TPU v7x, 256 devices: a whole 4x4x8 slice. The times are simulated.
256 devices in a mesh: tok: 64 (over z, x, core), grp: 4 (over y).
Axes of the slice: x: 4, y: 4, z: 8, core: 2. Of those that a mesh axis runs over, the one named last changes fastest.
Arguments:
- inputs: float32 [4, 8192, 1536], P('grp', 'tok'), may hold values from -6 to 6
- queries: bfloat16 [4, 8192, 1536], P('grp', 'tok'), may hold values from -100 to 100
- keys: bfloat16 [4, 8192, 256], P('grp', 'tok'), may hold values from -6 to 6
- values: bfloat16 [4, 8192, 256], P('grp', 'tok'), may hold values from -6 to 6
- prefix_keys: bfloat16 [2048, 256], P(('tok', 'grp')), may hold values from -7 to 7
- prefix_values: bfloat16 [2048, 256], P(('tok', 'grp')), may hold values from -6 to 6
- lengths: int32 [4, 16], replicated, may hold values from 1 to 4224, 8192 in all within a row
- out_weight: bfloat16 [1536, 1536], replicated, may hold values from -0.5 to 0.5
- norm_gain: float32 [1536], replicated, may hold values from 0.25 to 1.75
- router_weight: bfloat16 [1536, 32], replicated, may hold values from -0.15625 to 0.15625
- routes: int32 [4, 8192, 4], P('grp', 'tok'), may hold values from 0 to 31, all different within a row; in each aligned block of 128 rows (0 to 127, 128 to 255, ..., all dimensions but the last counted through in order) at most 24 rows name the same one
- expert_gate: bfloat16 [64, 1536, 384], P('tok'), may hold values from -0.15625 to 0.15625
- expert_up: bfloat16 [64, 1536, 384], P('tok'), may hold values from -0.15625 to 0.15625
- expert_down: bfloat16 [64, 384, 1536], P('tok'), may hold values from -0.21875 to 0.21875
Outputs:
- layer_out: float32 [4, 8192, 1536], P('grp', 'tok')
Inputs may be any that keep to these rules, and one draw needn't show every extreme that they name: Row g holds the suffix lengths of the 16 requests of group g, in order; they sum to 8192, and the longest is exactly 4224. `routes`: each token names 4 different experts; of one device's 128 tokens no more than 24 name one expert, and in every draw some expert is named by exactly 24 of them.
All inputs are finite; a program needn't handle non-finite values.
Results may differ from a plain program's by a relative error of at most 0.0055.
Values may be sent and summed in bfloat16 or wider, within the bound.
A program may use at most 192 MiB of HBM per device.

v0:
```python
import math
import jax
import jax.numpy as jnp
from jax import lax
from jax.sharding import PartitionSpec as P

HEADS = 12
KVH = 2
HD = 128
EXPERTS = 32
TOP = 4
CAP = 24
NEGATIVE = -1e30


def absorb(running, key_piece, value_piece, valid, query_heads):
    running_max, denominator, numerator = running
    key_count = key_piece.shape[0]
    key_heads = key_piece.reshape(key_count, KVH, HD)
    value_heads = value_piece.reshape(key_count, KVH, HD)
    scores = jnp.einsum(
        "tgrd,kgd->grtk", query_heads, key_heads, preferred_element_type=jnp.float32
    ) * (1.0 / math.sqrt(HD))
    if valid is None:
        masked = scores
    else:
        masked = jnp.where(valid[None, None], scores, NEGATIVE)
    new_max = jnp.maximum(running_max, jnp.max(masked, axis=-1))
    factor = jnp.exp(running_max - new_max)
    weights = jnp.exp(masked - new_max[..., None])
    if valid is not None:
        weights = jnp.where(valid[None, None], weights, 0.0)
    denominator = denominator * factor + jnp.sum(weights, axis=-1)
    numerator = numerator * factor[..., None] + jnp.einsum(
        "grtk,kgd->grtd",
        weights.astype(jnp.bfloat16),
        value_heads,
        preferred_element_type=jnp.float32,
    )
    return (new_max, denominator, numerator)


def local(
    inputs,
    queries,
    keys,
    values,
    prefix_keys,
    prefix_values,
    lengths,
    out_weight,
    norm_gain,
    router_weight,
    routes,
    expert_gate,
    expert_up,
    expert_down,
):
    tok_rows = queries.shape[1]
    model_width = out_weight.shape[1]
    repeat = HEADS // KVH
    query_heads = queries[0].reshape(tok_rows, KVH, repeat, HD)
    device = lax.axis_index("tok")
    positions = device * tok_rows + jnp.arange(tok_rows, dtype=jnp.int32)
    row_lengths = lax.dynamic_index_in_dim(lengths, lax.axis_index("grp"), 0, keepdims=False)
    request_ends = jnp.cumsum(row_lengths)
    starts = jnp.max(
        jnp.where(request_ends[None, :] <= positions[:, None], request_ends[None, :], 0), axis=1
    )
    softmax_state = (
        jnp.full((KVH, repeat, tok_rows), NEGATIVE, jnp.float32),
        jnp.zeros((KVH, repeat, tok_rows), jnp.float32),
        jnp.zeros((KVH, repeat, tok_rows, HD), jnp.float32),
    )
    shard_pair = (
        lax.all_gather(prefix_keys, ("tok", "grp"), axis=0, tiled=True),
        lax.all_gather(prefix_values, ("tok", "grp"), axis=0, tiled=True),
    )
    softmax_state = absorb(softmax_state, shard_pair[0], shard_pair[1], None, query_heads)
    own_keys = keys[0]
    own_values = values[0]
    shard_pair = (
        lax.all_gather(own_keys, "tok", axis=0, tiled=True),
        lax.all_gather(own_values, "tok", axis=0, tiled=True),
    )
    key_positions = jnp.arange(shard_pair[0].shape[0], dtype=jnp.int32)
    softmax_state = absorb(
        softmax_state,
        shard_pair[0],
        shard_pair[1],
        (key_positions[None, :] >= starts[:, None])
        & (key_positions[None, :] <= positions[:, None]),
        query_heads,
    )
    attended = (softmax_state[2] / softmax_state[1][..., None]).astype(jnp.bfloat16)
    attended = attended.transpose(2, 0, 1, 3).reshape(tok_rows, HEADS * HD)
    residual = inputs[0] + jnp.dot(attended, out_weight, preferred_element_type=jnp.float32)
    normed = (
        residual
        * lax.rsqrt(jnp.mean(residual * residual, axis=-1, keepdims=True) + 1e-06)
        * norm_gain
    ).astype(jnp.bfloat16)
    logits = jnp.dot(normed, router_weight, preferred_element_type=jnp.float32)
    token_routes = routes[0]
    sigmoids = jax.nn.sigmoid(jnp.take_along_axis(logits, token_routes, axis=1))
    gate_weights = sigmoids / jnp.sum(sigmoids, axis=1, keepdims=True)
    pair_experts = token_routes.reshape(-1)
    onehot = (pair_experts[:, None] == jnp.arange(EXPERTS, dtype=jnp.int32)[None, :]).astype(
        jnp.int32
    )
    slot_index = jnp.sum(jnp.cumsum(onehot, axis=0) * onehot, axis=1) - 1
    targets = pair_experts * CAP + slot_index
    buffer = (
        jnp.zeros((EXPERTS * CAP, model_width), jnp.bfloat16)
        .at[targets]
        .set(jnp.repeat(normed, TOP, axis=0))
    )
    local_slices = expert_gate.shape[0]
    tok_count = lax.axis_size("tok")
    split_count = local_slices * tok_count // EXPERTS
    outgoing = jnp.repeat(buffer.reshape(EXPERTS, CAP, model_width), split_count, axis=0).reshape(
        tok_count, local_slices, CAP, model_width
    )
    weight_sets = (expert_gate[:, None], expert_up[:, None], expert_down[:, None])
    arrived = lax.all_to_all(outgoing, "tok", split_axis=0, concat_axis=0, tiled=True)
    sources = arrived.shape[0]
    slot_count = arrived.shape[2]
    slot_rows = arrived[:, 0].reshape(sources * slot_count, model_width)
    gated = jax.nn.relu(
        jnp.dot(slot_rows, weight_sets[0][0, 0], preferred_element_type=jnp.float32)
    )
    hidden = (
        gated * jnp.dot(slot_rows, weight_sets[1][0, 0], preferred_element_type=jnp.float32)
    ).astype(jnp.bfloat16)
    part_out = jnp.dot(hidden, weight_sets[2][0, 0], preferred_element_type=jnp.float32).astype(
        jnp.bfloat16
    )
    total = lax.optimization_barrier(part_out).astype(jnp.float32)
    results = [total.astype(jnp.bfloat16).reshape(sources, slot_count, model_width)]
    computed = jnp.stack(results, axis=1)
    returned = lax.all_to_all(computed, "tok", split_axis=0, concat_axis=0, tiled=True)
    summed = jnp.sum(
        returned.reshape(EXPERTS, split_count, CAP, model_width).astype(jnp.float32), axis=1
    ).reshape(EXPERTS * CAP, model_width)
    expert_out = lax.optimization_barrier(summed.astype(jnp.bfloat16)).astype(jnp.float32)
    combined = jnp.sum(
        expert_out[targets].reshape(tok_rows, TOP, model_width) * gate_weights[:, :, None], axis=1
    )
    return (residual + combined)[None]


def solution(mesh):
    placed = (
        P("grp", "tok", None),
        P("grp", "tok", None),
        P("grp", "tok", None),
        P("grp", "tok", None),
        P(("tok", "grp"), None),
        P(("tok", "grp"), None),
        P(),
        P(),
        P(),
        P(),
        P("grp", "tok", None),
        P("tok", None, None),
        P("tok", None, None),
        P("tok", None, None),
    )
    return jax.shard_map(
        local, mesh=mesh, in_specs=placed, out_specs=P("grp", "tok", None), check_vma=False
    )
```

profile of v0, /device:TPU:8, one launch (start us, length us, event | category | flops | bytes accessed | tf_op | source)
XLA Modules:
  0.0 691.7 jit_solution(8346470615721139849)
XLA Ops:
  17.6 99.3 %all-gather.7.cloned.1.call-done = bf16[2048,256]{1,0:T(8,128)(2,1)} async-done(((bf16[8,256]{1,0:T(8,128)(2,1)}), bf16[2048,256]{1,0:T(8,128)(2,1)}) %all-gather.7.cloned.1.call-update) | async-done | bytes 1048592 | tf_op jit(solution)/shard_map/all_gather | solution.py:76
  118.4 7.3 %bitcast_reduce_fusion = (f32[2,6,128]{2,1,0:T(8,128)S(1)}, f32[2,2048,128,6]{2,1,3,0:T(8,128)}) fusion(bf16[2048,2,128,1]{0,2,3,1:T(8,128)(2,1)S(1)} %bitcast.168, bf16[128,2,6,128]{0,3,2,1:T(8,128)(2,1)} %bitcast.171), kind=kOutput, calls=%fused_computation.11 | convolution fusion | flops 811596288 | bytes 14030848 | tf_op jit(solution)/shard_map/tgrd,kgd->grtk/dot_general | solution.py:21
  125.7 96.9 %all-gather.9.cloned.1.call-done = bf16[2048,256]{1,0:T(8,128)(2,1)} async-done(((bf16[8,256]{1,0:T(8,128)(2,1)}), bf16[2048,256]{1,0:T(8,128)(2,1)}) %all-gather.9.cloned.1.call-update) | async-done | bytes 1048592 | tf_op jit(solution)/shard_map/all_gather | solution.py:77
  224.1 76.4 %all-gather.11.cloned.1.call-done = bf16[1,8192,256]{1,2,0:T(8,128)(2,1)} async-done(((bf16[1,128,256]{1,2,0:T(8,128)(2,1)}), bf16[1,8192,256]{1,2,0:T(8,128)(2,1)}) %all-gather.11.cloned.1.call-update) | async-done | bytes 4194320 | tf_op jit(solution)/shard_map/all_gather | solution.py:83
  300.4 21.5 %fusion = (f32[2,6,128]{2,1,0:T(8,128)S(1)}, f32[2,8192,128,6]{2,1,3,0:T(8,128)}) fusion(pred[128,8192]{0,1:T(8,128)(4,1)S(1)} %fusion.11, bf16[8192,2,128,1]{0,2,3,1:T(8,128)(2,1)} %bitcast.177, bf16[128,2,6,128]{0,3,2,1:T(8,128)(2,1)} %bitcast.172), kind=kOutput, calls=%fused_computation.5 | convolution fusion | flops 3258972672 | bytes 55973888 | tf_op jit(solution)/shard_map/tgrd,kgd->grtk/dot_general | solution.py:21
  321.9 6.8 fusion.7
  328.8 23.4 %fusion.1 = f32[2,6,128]{2,1,0:T(8,128)S(1)} fusion(f32[2,8192,128,6]{2,1,3,0:T(8,128)} %get-tuple-element.11, f32[2,6,128]{2,1,0:T(8,128)S(1)} %get-tuple-element.8, pred[128,8192]{0,1:T(8,128)(4,1)S(1)} %fusion.11), kind=kLoop, calls=%fused_computation.6 | loop fusion | flops 62913024 | bytes 51392512 | tf_op jit(solution)/shard_map/reduce_sum | solution.py:33
  352.2 3.3 fusion.25
  355.5 26.0 %all-gather.13.cloned.1.call-done = bf16[1,8192,256]{2,1,0:T(8,128)(2,1)} async-done(((bf16[1,128,256]{2,1,0:T(8,128)(2,1)}), bf16[1,8192,256]{2,1,0:T(8,128)(2,1)}) %all-gather.13.cloned.1.call-update) | async-done | bytes 4194320 | tf_op jit(solution)/shard_map/all_gather | solution.py:84
  381.5 6.3 copy.89
  387.8 20.6 %fusion.36 = bf16[128,2,6,128]{0,3,2,1:T(8,128)(2,1)S(1)} fusion(f32[128,2,6,128]{0,3,2,1:T(8,128)} %fusion.25, bf16[8192,2,128,1]{0,2,3,1:T(8,128)(2,1)} %bitcast.169, f32[2,8192,128,6]{2,1,3,0:T(8,128)} %get-tuple-element.11, f32[2,6,128]{2,1,0:T(8,128)S(1)} %get-tuple-element.8, pred[128,8192]{0,1:T(8,128)(4,1)S(1)} %fusion.11, ...), kind=kOutput, calls=%fused_computation.37 | convolution fusion | flops 3284729856 | bytes 56766464 | tf_op jit(solution)/shard_map/grtk,kgd->grtd/dot_general | solution.py:34
  408.5 3.2 multiply_reduce_fusion.1
  415.2 4.6 scatter_custom_fusion
  420.2 113.8 %all_to_all.10 = bf16[64,1,24,1536]{3,2,1,0:T(8,128)(2,1)S(1)} all-to-all(bf16[64,1,24,1536]{3,2,1,0:T(8,128)(2,1)S(1)} %bitcast.162), channel_id=1, replica_groups=mesh['tok'=64,'grp'=4] {'tok'}, dimensions={0} | all-to-all | bytes 9437184 | tf_op jit(solution)/shard_map/all_to_all | solution.py:125
  536.2 4.0 convolution_maximum_fusion
  540.2 8.6 %convolution_convert_fusion = bf16[1536,1536]{1,0:T(8,128)(2,1)} fusion(bf16[1,384,1536]{2,1,0:T(8,128)(2,1)S(1)} %copy-done, f32[1536,384]{1,0:T(8,128)} %convolution_maximum_fusion, bf16[1536,1536]{1,0:T(8,128)(2,1)} %bitcast.167, bf16[1,1536,384]{2,1,0:T(8,128)(2,1)S(1)} %copy-done.11), kind=kOutput, calls=%fused_computation.15 | convolution fusion | flops 3627417600 | bytes 14155776 | tf_op jit(solution)/shard_map/dot_general | solution.py:135
  548.8 6.1 all-to-all-start.1
  555.4 3.8 gather_fusion.1
  559.5 102.9 %all-to-all-done.1 = bf16[64,1,24,1536]{3,2,1,0:T(8,128)(2,1)} async-done(((bf16[64,1,24,1536]{3,2,1,0:T(8,128)(2,1)}), bf16[64,1,24,1536]{3,2,1,0:T(8,128)(2,1)}, u32[]{:S(2)}, u32[]{:S(2)}) %all-to-all-start.1) | async-done | bytes 4718624 | tf_op jit(solution)/shard_map/all_to_all | solution.py:141
  662.5 3.0 bitcast_reduce_fusion.1
  665.5 2.8 convert_element_type.56
  668.3 6.9 gather_fusion
  675.2 4.9 reshape.263
  680.0 4.2 multiply_reduce_fusion
  (82 shorter events, 21.8 us)
Async XLA Ops:
  6.5 533.6 %copy-start = (bf16[1,384,1536]{2,1,0:T(8,128)(2,1)S(1)}, bf16[1,384,1536]{2,1,0:T(8,128)(2,1)}, u32[]{:S(2)}) copy-start(bf16[1,384,1536]{2,1,0:T(8,128)(2,1)} %param.27) | copy-start | bytes 3538948
  6.5 110.3 %all-gather.7.cloned.1.call-start = ((), (), s32[]{:S(2)}) async-start(), calls=%async_computation.2 | async-start | bytes 1052672 | tf_op jit(solution)/shard_map/all_gather | solution.py:76
  7.3 215.3 %all-gather.9.cloned.1.call-start = ((), (), s32[]{:S(2)}) async-start(), calls=%async_computation.3 | async-start | bytes 1052672 | tf_op jit(solution)/shard_map/all_gather | solution.py:77
  8.0 292.4 %all-gather.11.cloned.1.call-start = ((), (), s32[]{:S(2)}) async-start(), calls=%async_computation.4 | async-start | bytes 4259840 | tf_op jit(solution)/shard_map/all_gather | solution.py:83
  9.6 371.8 %all-gather.13.cloned.1.call-start = ((), (), s32[]{:S(2)}) async-start(), calls=%async_computation.5 | async-start | bytes 4259840 | tf_op jit(solution)/shard_map/all_gather | solution.py:84
  321.9 30.2 %slice-start = ((s8[12582912]{0:T(1024)(128)(4,1)}), s8[4194304]{0:T(1024)(128)(4,1)S(1)}, s32[]{:S(2)}) async-start(s8[12582912]{0:T(1024)(128)(4,1)} %bitcast.160), calls=%async_computation.6 | async-start | bytes 8388608
  328.7 23.4 %slice-start.1 = ((s8[12582912]{0:T(1024)(128)(4,1)}), s8[4194304]{0:T(1024)(128)(4,1)S(1)}, s32[]{:S(2)}) async-start(s8[12582912]{0:T(1024)(128)(4,1)} %bitcast.160), calls=%async_computation.7 | async-start | bytes 8388608
  328.7 23.4 %slice-start.2 = ((s8[12582912]{0:T(1024)(128)(4,1)}), s8[4194304]{0:T(1024)(128)(4,1)S(1)}, s32[]{:S(2)}) async-start(s8[12582912]{0:T(1024)(128)(4,1)} %bitcast.160), calls=%async_computation.8 | async-start | bytes 8388608
  387.8 20.6 %copy-start.6 = (f32[1,128,1536]{2,1,0:T(8,128)S(1)}, f32[1,128,1536]{2,1,0:T(8,128)}, u32[]{:S(2)}) copy-start(f32[1,128,1536]{2,1,0:T(8,128)} %param.14) | copy-start | bytes 2359300
  408.4 4.1 copy-start.9
  411.7 0.9 copy-start.1
  412.7 0.7 copy-start.4
  420.2 115.9 %copy-start.10 = (bf16[1,1536,384]{2,1,0:T(8,128)(2,1)S(1)}, bf16[1,1536,384]{2,1,0:T(8,128)(2,1)}, u32[]{:S(2)}) copy-start(bf16[1,1536,384]{2,1,0:T(8,128)(2,1)} %param.25) | copy-start | bytes 3538948
  534.0 2.2 copy-start.3
  536.2 4.0 copy-start.11
  548.8 6.1 copy-start.8
  548.8 6.4 copy-start.5
  548.8 6.4 copy-start.7
  548.8 113.7 %all-to-all-start.1 = ((bf16[64,1,24,1536]{3,2,1,0:T(8,128)(2,1)}), bf16[64,1,24,1536]{3,2,1,0:T(8,128)(2,1)}, u32[]{:S(2)}, u32[]{:S(2)}) async-start(bf16[64,1,24,1536]{3,2,1,0:T(8,128)(2,1)} %bitcast.165), calls=%async_computation.1 | async-start | bytes 9437184 | tf_op jit(solution)/shard_map/all_to_all | solution.py:141
  675.2 9.0 %copy-start.2 = (f32[128,1536]{1,0:T(8,128)S(1)}, f32[128,1536]{1,0:T(8,128)}, u32[]{:S(2)}) copy-start(f32[128,1536]{1,0:T(8,128)} %copy-done.1) | copy-start | bytes 2359300
Sparse Core Ops, SparseCore 0:
  11.1 105.7 all-gather.6
  120.6 101.9 all-gather.8
  225.2 75.1 all-gather.10
  303.1 78.3 all-gather.12
where the time goes:
time: 693 us; the launch traced here: 692 us
  waiting for transfers between devices  403 us (58%)
  blocking collectives  114 us (16%)
  matrix products  68.7 us (10%)
  other arithmetic  44.6 us (6%)
  local copies, waits for them, and re-layouts  41.6 us (6%)
  between operations  13.5 us (2%)
    all_to_all x1, blocking collectives, local(): lax.all_to_all(outgoing, 'tok', split_axis=0, concat_axis=0, tiled=True)  114 us
    all_to_all x1, waiting for transfers between devices, local(): lax.all_to_all(computed, 'tok', split_axis=0, concat_axis=0, tiled=True)  103 us
    all_gather x1, waiting for transfers between devices, local(): lax.all_gather(prefix_keys, ('tok', 'grp'), axis=0, tiled=True)  99.3 us
    all_gather x1, waiting for transfers between devices, local(): lax.all_gather(prefix_values, ('tok', 'grp'), axis=0, tiled=True)  96.9 us
    all_gather x1, waiting for transfers between devices, local(): lax.all_gather(own_keys, 'tok', axis=0, tiled=True)  76.4 us
    reduce_sum x2, other arithmetic, absorb(): denominator = denominator * factor + jnp.sum(weights, axis=-1)  30.2 us
    dot_general x2, matrix products, absorb(): jnp.einsum('tgrd,kgd->grtk', query_heads, key_heads, preferred_element_ty...  28.8 us
    all_gather x1, waiting for transfers between devices, local(): lax.all_gather(own_values, 'tok', axis=0, tiled=True)  26 us
  transfers between devices with their start and end apart: 5, of which 5 were waited for; matrix products, arithmetic and copies ran while one was open for 11% of the time, Pallas kernels for 0%

commit v1 on v0

--- a/solution.py
+++ b/solution.py
@@ -3,6 +3,7 @@
 import jax.numpy as jnp
 from jax import lax
 from jax.sharding import PartitionSpec as P
+from jax.lax import all_to_all, axis_size
 
 HEADS = 12
 KVH = 2
@@ -79,10 +80,15 @@
     softmax_state = absorb(softmax_state, shard_pair[0], shard_pair[1], None, query_heads)
     own_keys = keys[0]
     own_values = values[0]
-    shard_pair = (
-        lax.all_gather(own_keys, "tok", axis=0, tiled=True),
-        lax.all_gather(own_values, "tok", axis=0, tiled=True),
-    )
+
+    def _update_shards(mine):
+        pieces_in = []
+        for _ in range(axis_size("tok")):
+            pieces_in.append(mine)
+        formed = jnp.concatenate(all_to_all(jnp.stack(pieces_in), "tok", 0, 0), 0)
+        return formed
+
+    shard_pair = (_update_shards(own_keys), lax.all_gather(own_values, "tok", axis=0, tiled=True))
     key_positions = jnp.arange(shard_pair[0].shape[0], dtype=jnp.int32)
     softmax_state = absorb(
         softmax_state,

time: 693 us -> 647 us (0.934); the launches traced: 692 us -> 637 us
  waiting for transfers between devices: 403 us -> 320 us
  local copies, waits for them, and re-layouts: 41.6 us -> 57.6 us
  starting transfers between devices: 6.25 us -> 18.8 us
    all_gather x1 -> x0, waiting for transfers between devices: 76.4 us -> none  [local(): lax.all_gather(own_keys, 'tok', axis=0, tiled=True)]
    all_gather x1, waiting for transfers between devices: 26 us -> 1.72 us  [local(): lax.all_gather(own_values, 'tok', axis=0, tiled=True)]
    all_to_all x0 -> x1, starting transfers between devices: none -> 12.3 us  [_update_shards(): formed = jnp.concatenate(all_to_all(jnp.stack(pieces_in), 'tok', 0, 0), 0)]
    another operation x3 -> x6, local copies, waits for them, and re-layouts: 0.78 us -> 12.2 us  [the longest x1 7.36 us: absorb(): key_heads = key_piece.reshape(key_count, KVH, HD)]
    all_gather x1, waiting for transfers between devices: 99.3 us -> 109 us  [local(): lax.all_gather(prefix_keys, ('tok', 'grp'), axis=0, tiled=True)]
    all_gather x1, waiting for transfers between devices: 96.9 us -> 104 us  [local(): lax.all_gather(prefix_values, ('tok', 'grp'), axis=0, tiled=True)]
  transfers between devices with their start and end apart: 5 -> 5, of which waited for: 5 -> 4; matrix products, arithmetic and copies ran while one was open for 11% -> 14% of each run, Pallas kernels for 0% -> 0%
where the time goes in v1:
time: 647 us; the launch traced here: 637 us
  waiting for transfers between devices  320 us (49%)
  blocking collectives  114 us (18%)
  matrix products  68.6 us (11%)
  local copies, waits for them, and re-layouts  57.6 us (9%)
  other arithmetic  44.3 us (7%)
  starting transfers between devices  18.8 us (3%)
  between operations  13.7 us (2%)
    all_to_all x1, blocking collectives, local(): lax.all_to_all(outgoing, 'tok', split_axis=0, concat_axis=0, tiled=True)  114 us
    all_gather x1, waiting for transfers between devices, local(): lax.all_gather(prefix_keys, ('tok', 'grp'), axis=0, tiled=True)  109 us
    all_gather x1, waiting for transfers between devices, local(): lax.all_gather(prefix_values, ('tok', 'grp'), axis=0, tiled=True)  104 us
    all_to_all x1, waiting for transfers between devices, local(): lax.all_to_all(computed, 'tok', split_axis=0, concat_axis=0, tiled=True)  103 us
    reduce_sum x2, other arithmetic, absorb(): denominator = denominator * factor + jnp.sum(weights, axis=-1)  30.5 us
    dot_general x2, matrix products, absorb(): jnp.einsum('tgrd,kgd->grtk', query_heads, key_heads, preferred_element_ty...  28.7 us
    dot_general x2, matrix products, absorb(): jnp.einsum('grtk,kgd->grtd', weights.astype(jnp.bfloat16), value_heads, p...  23.9 us
  transfers between devices with their start and end apart: 5, of which 4 were waited for; matrix products, arithmetic and copies ran while one was open for 14% of the time, Pallas kernels for 0%

profile of v1, /device:TPU:8, one launch (start us, length us, event | category | flops | bytes accessed | tf_op | source)
XLA Modules:
  0.0 636.9 jit_solution(533115357203324467)
XLA Ops:
  10.6 12.3 %all-to-all-start = ((bf16[64,128,256]{1,2,0:T(8,128)(2,1)}), bf16[64,128,256]{1,2,0:T(8,128)(2,1)}, u32[]{:S(2)}, u32[]{:S(2)}) async-start(bf16[64,128,256]{1,2,0:T(8,128)(2,1)} %stack.3), calls=%async_computation | async-start | bytes 8388608 | tf_op jit(solution)/shard_map/all_to_all | solution.py:88
  30.2 108.7 %all-gather.5.cloned.1.call-done = bf16[2048,256]{1,0:T(8,128)(2,1)} async-done(((bf16[8,256]{1,0:T(8,128)(2,1)}), bf16[2048,256]{1,0:T(8,128)(2,1)}) %all-gather.5.cloned.1.call-update) | async-done | bytes 1048592 | tf_op jit(solution)/shard_map/all_gather | solution.py:77
  140.4 104.4 %all-gather.7.cloned.1.call-done = bf16[2048,256]{1,0:T(8,128)(2,1)} async-done(((bf16[8,256]{1,0:T(8,128)(2,1)}), bf16[2048,256]{1,0:T(8,128)(2,1)}) %all-gather.7.cloned.1.call-update) | async-done | bytes 1048592 | tf_op jit(solution)/shard_map/all_gather | solution.py:78
  247.0 7.3 %bitcast_reduce_fusion = (f32[2,6,128]{2,1,0:T(8,128)S(1)}, f32[2,2048,128,6]{2,1,3,0:T(8,128)}) fusion(bf16[2048,2,128,1]{0,2,3,1:T(8,128)(2,1)S(1)} %bitcast.172, bf16[128,2,6,128]{0,3,2,1:T(8,128)(2,1)} %bitcast.175), kind=kOutput, calls=%fused_computation.11 | convolution fusion | flops 811596288 | bytes 14030848 | tf_op jit(solution)/shard_map/tgrd,kgd->grtk/dot_general | solution.py:22
  254.3 6.9 %copy.89 = bf16[64,128,256]{1,0,2:T(8,128)(2,1)} copy(bf16[64,128,256]{1,2,0:T(8,128)(2,1)} %all-to-all-done) | data formatting | bytes 8388608 | tf_op jit(solution)/shard_map/all_to_all | solution.py:88
  261.2 7.4 %reshape_reshape.6 = bf16[8192,2,128]{0,2,1:T(8,128)(2,1)} reshape(bf16[64,128,256]{1,0,2:T(8,128)(2,1)} %copy.89) | data formatting | bytes 8388608 | tf_op jit(solution)/shard_map/reshape;reshape | solution.py:20
  268.5 21.4 %fusion = (f32[2,6,128]{2,1,0:T(8,128)S(1)}, f32[2,8192,128,6]{2,1,3,0:T(8,128)}) fusion(pred[128,8192]{0,1:T(8,128)(4,1)S(1)} %fusion.13, bf16[128,2,6,128]{0,3,2,1:T(8,128)(2,1)S(1)} %bitcast.176, bf16[8192,2,128]{0,2,1:T(8,128)(2,1)} %reshape_reshape.6), kind=kOutput, calls=%fused_computation.5 | convolution fusion | flops 3258972672 | bytes 55973888 | tf_op jit(solution)/shard_map/tgrd,kgd->grtk/dot_general | solution.py:22
  289.9 6.8 %fusion.7 = f32[2,6,128]{2,1,0:T(8,128)S(1)} fusion(f32[2,2048,128,6]{2,1,3,0:T(8,128)} %get-tuple-element.13, f32[2,6,128]{2,1,0:T(8,128)S(1)} %get-tuple-element.9), kind=kLoop, calls=%fused_computation.13 | loop fusion | flops 9435648 | bytes 12595200 | tf_op jit(solution)/shard_map/reduce_sum | solution.py:34
  296.8 23.8 %fusion.1 = f32[2,6,128]{2,1,0:T(8,128)S(1)} fusion(f32[2,8192,128,6]{2,1,3,0:T(8,128)} %get-tuple-element.11, f32[2,6,128]{2,1,0:T(8,128)S(1)} %get-tuple-element.8, pred[128,8192]{0,1:T(8,128)(4,1)S(1)} %fusion.13), kind=kLoop, calls=%fused_computation.6 | loop fusion | flops 62913024 | bytes 51392512 | tf_op jit(solution)/shard_map/reduce_sum | solution.py:34
  320.6 3.3 fusion.27
  325.6 6.3 copy.92
  331.9 20.6 %fusion.38 = bf16[128,2,6,128]{0,3,2,1:T(8,128)(2,1)S(1)} fusion(f32[128,2,6,128]{0,3,2,1:T(8,128)} %fusion.27, bf16[8192,2,128,1]{0,2,3,1:T(8,128)(2,1)} %bitcast.173, f32[2,8192,128,6]{2,1,3,0:T(8,128)} %get-tuple-element.11, f32[2,6,128]{2,1,0:T(8,128)S(1)} %get-tuple-element.8, pred[128,8192]{0,1:T(8,128)(4,1)S(1)} %fusion.13, ...), kind=kOutput, calls=%fused_computation.39 | convolution fusion | flops 3284729856 | bytes 56766464 | tf_op jit(solution)/shard_map/grtk,kgd->grtd/dot_general | solution.py:35
  352.6 3.2 multiply_reduce_fusion.1
  359.4 4.8 scatter_custom_fusion
  364.5 114.2 %all_to_all.15 = bf16[64,1,24,1536]{3,2,1,0:T(8,128)(2,1)S(1)} all-to-all(bf16[64,1,24,1536]{3,2,1,0:T(8,128)(2,1)S(1)} %bitcast.166), channel_id=1, replica_groups=mesh['tok'=64,'grp'=4] {'tok'}, dimensions={0} | all-to-all | bytes 9437184 | tf_op jit(solution)/shard_map/all_to_all | solution.py:131
  480.9 4.0 convolution_maximum_fusion
  484.9 8.6 %convolution_convert_fusion = bf16[1536,1536]{1,0:T(8,128)(2,1)} fusion(bf16[1,384,1536]{2,1,0:T(8,128)(2,1)S(1)} %copy-done, f32[1536,384]{1,0:T(8,128)} %convolution_maximum_fusion, bf16[1536,1536]{1,0:T(8,128)(2,1)} %bitcast.171, bf16[1,1536,384]{2,1,0:T(8,128)(2,1)S(1)} %copy-done.14), kind=kOutput, calls=%fused_computation.15 | convolution fusion | flops 3627417600 | bytes 14155776 | tf_op jit(solution)/shard_map/dot_general | solution.py:141
  493.5 6.3 all-to-all-start.2
  500.3 3.8 gather_fusion.1
  504.4 102.9 %all-to-all-done.2 = bf16[64,1,24,1536]{3,2,1,0:T(8,128)(2,1)} async-done(((bf16[64,1,24,1536]{3,2,1,0:T(8,128)(2,1)}), bf16[64,1,24,1536]{3,2,1,0:T(8,128)(2,1)}, u32[]{:S(2)}, u32[]{:S(2)}) %all-to-all-start.2) | async-done | bytes 4718624 | tf_op jit(solution)/shard_map/all_to_all | solution.py:147
  607.4 3.0 bitcast_reduce_fusion.1
  613.2 6.9 %gather_fusion = f32[512,1536]{1,0:T(8,128)} fusion(f32[768,1536]{1,0:T(8,128)} %convert_element_type.56, s32[1024]{0:T(1024)S(1)} %pad_clamp_fusion), kind=kCustom, calls=%fused_computation | custom fusion | bytes 6293504 | tf_op jit(solution)/shard_map/gather | solution.py:153
  620.1 4.9 reshape.260
  624.9 4.2 multiply_reduce_fusion
  (90 shorter events, 27.3 us)
Async XLA Ops:
  6.5 478.4 %copy-start = (bf16[1,384,1536]{2,1,0:T(8,128)(2,1)S(1)}, bf16[1,384,1536]{2,1,0:T(8,128)(2,1)}, u32[]{:S(2)}) copy-start(bf16[1,384,1536]{2,1,0:T(8,128)(2,1)} %param.27) | copy-start | bytes 3538948
  10.6 14.6 %copy-start.11 = (s32[1,128,4]{1,2,0:T(4,128)S(1)}, s32[1,128,4]{1,2,0:T(4,128)}, u32[]{:S(2)}) copy-start(s32[1,128,4]{1,2,0:T(4,128)} %param.24) | copy-start | bytes 6148
  10.6 15.8 %copy-start.9 = (bf16[1,128,1536]{2,1,0:T(8,128)(2,1)S(1)}, bf16[1,128,1536]{2,1,0:T(8,128)(2,1)}, u32[]{:S(2)}) copy-start(bf16[1,128,1536]{2,1,0:T(8,128)(2,1)} %param.15) | copy-start | bytes 1179652
  10.6 243.7 %all-to-all-start = ((bf16[64,128,256]{1,2,0:T(8,128)(2,1)}), bf16[64,128,256]{1,2,0:T(8,128)(2,1)}, u32[]{:S(2)}, u32[]{:S(2)}) async-start(bf16[64,128,256]{1,2,0:T(8,128)(2,1)} %stack.3), calls=%async_computation | async-start | bytes 8388608 | tf_op jit(solution)/shard_map/all_to_all | solution.py:88
  22.9 115.9 %all-gather.5.cloned.1.call-start = ((), (), s32[]{:S(2)}) async-start(), calls=%async_computation.3 | async-start | bytes 1052672 | tf_op jit(solution)/shard_map/all_gather | solution.py:77
  23.7 221.1 %all-gather.7.cloned.1.call-start = ((), (), s32[]{:S(2)}) async-start(), calls=%async_computation.4 | async-start | bytes 1052672 | tf_op jit(solution)/shard_map/all_gather | solution.py:78
  24.4 301.2 %all-gather.9.cloned.1.call-start = ((), (), s32[]{:S(2)}) async-start(), calls=%async_computation.5 | async-start | bytes 4259840 | tf_op jit(solution)/shard_map/all_gather | solution.py:91
  261.2 7.4 %copy-start.7 = (bf16[1,128,1536]{1,2,0:T(8,128)(2,1)S(1)}, bf16[1,128,1536]{1,2,0:T(8,128)(2,1)}, u32[]{:S(2)}) copy-start(bf16[1,128,1536]{1,2,0:T(8,128)(2,1)} %copy.82) | copy-start | bytes 1179652
  289.9 30.6 %slice-start = ((s8[12582912]{0:T(1024)(128)(4,1)}), s8[4194304]{0:T(1024)(128)(4,1)S(1)}, s32[]{:S(2)}) async-start(s8[12582912]{0:T(1024)(128)(4,1)} %bitcast.164), calls=%async_computation.6 | async-start | bytes 8388608
  296.7 23.8 %slice-start.1 = ((s8[12582912]{0:T(1024)(128)(4,1)}), s8[4194304]{0:T(1024)(128)(4,1)S(1)}, s32[]{:S(2)}) async-start(s8[12582912]{0:T(1024)(128)(4,1)} %bitcast.164), calls=%async_computation.7 | async-start | bytes 8388608
  296.7 23.8 %slice-start.2 = ((s8[12582912]{0:T(1024)(128)(4,1)}), s8[4194304]{0:T(1024)(128)(4,1)S(1)}, s32[]{:S(2)}) async-start(s8[12582912]{0:T(1024)(128)(4,1)} %bitcast.164), calls=%async_computation.8 | async-start | bytes 8388608
  296.8 23.8 %copy-start.4 = (bf16[2048,256]{0,1:T(8,128)(2,1)S(1)}, bf16[2048,256]{0,1:T(8,128)(2,1)}, u32[]{:S(2)}) copy-start(bf16[2048,256]{0,1:T(8,128)(2,1)} %copy.85) | copy-start | bytes 3145732
  331.9 20.6 %copy-start.8 = (f32[1,128,1536]{2,1,0:T(8,128)S(1)}, f32[1,128,1536]{2,1,0:T(8,128)}, u32[]{:S(2)}) copy-start(f32[1,128,1536]{2,1,0:T(8,128)} %param.14) | copy-start | bytes 2359300
  352.6 4.1 copy-start.12
  355.8 0.9 copy-start.1
  356.9 0.7 copy-start.5
  364.5 116.3 %copy-start.13 = (bf16[1,1536,384]{2,1,0:T(8,128)(2,1)S(1)}, bf16[1,1536,384]{2,1,0:T(8,128)(2,1)}, u32[]{:S(2)}) copy-start(bf16[1,1536,384]{2,1,0:T(8,128)(2,1)} %param.25) | copy-start | bytes 3538948
  478.7 2.2 copy-start.3
  480.9 4.0 copy-start.14
  493.5 6.6 %copy-start.6 = (bf16[128,1536]{1,0:T(8,128)(2,1)S(1)}, bf16[128,1536]{1,0:T(8,128)(2,1)}, u32[]{:S(2)}) copy-start(bf16[128,1536]{1,0:T(8,128)(2,1)} %copy-done.5) | copy-start | bytes 1179652
  493.5 6.6 %copy-start.10 = (bf16[1536,32]{0,1:T(8,128)(2,1)S(1)}, bf16[1536,32]{0,1:T(8,128)(2,1)}, u32[]{:S(2)}) copy-start(bf16[1536,32]{0,1:T(8,128)(2,1)} %param.23) | copy-start | bytes 294916
  493.5 113.9 %all-to-all-start.2 = ((bf16[64,1,24,1536]{3,2,1,0:T(8,128)(2,1)}), bf16[64,1,24,1536]{3,2,1,0:T(8,128)(2,1)}, u32[]{:S(2)}, u32[]{:S(2)}) async-start(bf16[64,1,24,1536]{3,2,1,0:T(8,128)(2,1)} %bitcast.169), calls=%async_computation.2 | async-start | bytes 9437184 | tf_op jit(solution)/shard_map/all_to_all | solution.py:147
  620.1 9.0 %copy-start.2 = (f32[128,1536]{1,0:T(8,128)S(1)}, f32[128,1536]{1,0:T(8,128)}, u32[]{:S(2)}) copy-start(f32[128,1536]{1,0:T(8,128)} %copy-done.1) | copy-start | bytes 2359300
Sparse Core Ops, SparseCore 0:
  27.5 111.3 all-gather.4
  142.6 102.0 all-gather.6
  247.5 78.0 all-gather.8
